TPU v7x, 32 devices: a whole 2x2x4 slice. The times are simulated.
32 devices in a mesh: dp: 8 (over z, x), ctx: 4 (over y, core).
Axes of the slice: x: 2, y: 2, z: 4, core: 2. Of those that a mesh axis runs over, the one named last changes fastest.
Arguments:
- tokens: bfloat16 [4096, 1024], P(('dp', 'ctx')), may hold values from -6 to 6
- cotangent: bfloat16 [4096, 1024], P(('dp', 'ctx')), may hold values from -6 to 6
- segment_ids: int32 [8, 512], P('dp'), may hold values from 0 to 3, never falling along the last dimension, each value on 1 to 256 neighbouring positions
- tract_order: int32 [8, 8], P('dp'), may hold values from 0 to 7, each once within a row
- qkv_weight: bfloat16 [1024, 3072], P(('dp', 'ctx')), may hold values from -0.1875 to 0.1875
- out_weight: bfloat16 [1024, 1024], P(('dp', 'ctx')), may hold values from -2 to 2
- up_weight: bfloat16 [1024, 4096], P(('dp', 'ctx')), may hold values from -0.1875 to 0.1875
- down_weight: bfloat16 [4096, 1024], P(('dp', 'ctx')), may hold values from -0.09375 to 0.09375
- norm_gain: bfloat16 [2, 1024], P(None, ('dp', 'ctx')), may hold values from 0.5 to 1.5
- norm_shift: bfloat16 [2, 1024], P(None, ('dp', 'ctx')), may hold values from -4 to 4
- proj_bias: bfloat16 [4, 1024], P(None, ('dp', 'ctx')), may hold values from -6 to 6
- up_bias: bfloat16 [4096], P(('dp', 'ctx')), may hold values from -6 to 6
Outputs:
- block_out: float32 [4096, 1024], P(('dp', 'ctx'))
- input_grad: float32 [4096, 1024], P(('dp', 'ctx'))
- qkv_weight_grad: float32 [1024, 3072], P(('dp', 'ctx'))
- out_weight_grad: float32 [1024, 1024], P(('dp', 'ctx'))
- up_weight_grad: float32 [1024, 4096], P(('dp', 'ctx'))
- down_weight_grad: float32 [4096, 1024], P(('dp', 'ctx'))
- norm_gain_grad: float32 [2, 1024], P(None, ('dp', 'ctx'))
- norm_shift_grad: float32 [2, 1024], P(None, ('dp', 'ctx'))
- proj_bias_grad: float32 [4, 1024], P(None, ('dp', 'ctx'))
- up_bias_grad: float32 [4096], P(('dp', 'ctx'))
Inputs may be any that keep to these rules, and one draw needn't show every extreme that they name: `segment_ids`: along each row the ids never fall; one document covers at most 256 positions of a row. `tract_order`: each row is a permutation: every place 0 to 7 is named once.
All inputs are finite; a program needn't handle non-finite values.
Results may differ from a plain program's by a relative error of at most 0.011.
Values may be sent and summed in bfloat16 or wider, within the bound.
A program may use at most 256 MiB of HBM per device.

v0:
```python
import jax
import jax.numpy as jnp
from jax import lax
from jax.sharding import PartitionSpec as P

HEAD_DIM = 64
EPSILON = 1e-05
GELU_COEF = 0.7978845608028654


def gelu_parts(inputs):
    cubed_part = inputs * inputs * inputs
    tanh_part = jnp.tanh(GELU_COEF * (inputs + 0.044715 * cubed_part))
    values = 0.5 * inputs * (1.0 + tanh_part)
    slopes = 0.5 * (1.0 + tanh_part) + 0.5 * inputs * (1.0 - tanh_part * tanh_part) * GELU_COEF * (
        1.0 + 3.0 * 0.044715 * inputs * inputs
    )
    return (values, slopes)


def norm_parts(values):
    centred = values - jnp.mean(values, axis=-1, keepdims=True)
    inverse = lax.rsqrt(jnp.mean(centred * centred, axis=-1, keepdims=True) + EPSILON)
    return (centred * inverse, inverse)


def norm_back(grads, normed, inverse, gain_row):
    scaled = grads * gain_row
    return inverse * (
        scaled
        - jnp.mean(scaled, axis=-1, keepdims=True)
        - normed * jnp.mean(scaled * normed, axis=-1, keepdims=True)
    )


def outer_sum(former, latter):
    return lax.dot_general(
        former, latter, (((0,), (0,)), ((), ())), preferred_element_type=jnp.float32
    )


def back_product(former, latter):
    return lax.dot_general(
        former, latter, (((1,), (1,)), ((), ())), preferred_element_type=jnp.float32
    )


def shards(
    tokens,
    cotangent,
    segment_ids,
    tract_order,
    qkv_weight,
    out_weight,
    up_weight,
    down_weight,
    norm_gain,
    norm_shift,
    proj_bias,
    up_bias,
):
    both = ("dp", "ctx")
    dp_count = lax.axis_size("dp")
    ctx_count = lax.axis_size("ctx")
    here = lax.axis_index("ctx")
    row_count, width = tokens.shape
    span = row_count * ctx_count
    block_rows = segment_ids.shape[1] // tract_order.shape[1]
    own_rows = qkv_weight.shape[0]
    own_hidden = up_bias.shape[0]
    own_feats = norm_gain.shape[1]
    hidden = dp_count * own_hidden
    part = width // ctx_count
    heads = part // HEAD_DIM
    attn_scale = HEAD_DIM ** (-0.5)
    smalls = jnp.concatenate(
        [norm_gain.reshape(-1), norm_shift.reshape(-1), proj_bias.reshape(-1), up_bias]
    )[None]
    smalls = lax.all_gather(smalls, both, axis=0, tiled=True).astype(jnp.float32)

    def spread(first, count):
        piece = smalls[:, first * own_feats : (first + count) * own_feats]
        return piece.reshape(-1, count, own_feats).transpose(1, 0, 2).reshape(count, width)

    gains = spread(0, 2)
    shifts = spread(2, 2)
    biases = spread(4, 4)
    up_shift = lax.dynamic_index_in_dim(
        smalls[:, 8 * own_feats :].reshape(dp_count, ctx_count, own_hidden), here, 1, False
    ).reshape(hidden)
    qkv_cols = (
        qkv_weight.reshape(own_rows, 3, ctx_count, part)
        .transpose(2, 0, 1, 3)
        .reshape(ctx_count, own_rows, 3 * part)
    )
    up_cols = (
        up_weight.reshape(own_rows, dp_count, ctx_count, own_hidden)
        .transpose(2, 0, 1, 3)
        .reshape(ctx_count, own_rows, hidden)
    )
    swapped = lax.all_to_all(
        jnp.concatenate([qkv_cols, up_cols], axis=2), "ctx", 0, 0, tiled=True
    ).reshape(ctx_count * own_rows, 3 * part + hidden)
    streams = lax.all_gather(jnp.stack([tokens, cotangent]), "ctx", axis=1, tiled=True)
    qkv_part = lax.all_gather(swapped[:, : 3 * part], "dp", axis=0, tiled=True)
    out_full = lax.all_gather(out_weight, both, axis=0, tiled=True)
    up_part = lax.all_gather(swapped[:, 3 * part :], "dp", axis=0, tiled=True)
    down_part = lax.all_gather(down_weight, "dp", axis=0, tiled=True)
    tokens_span, cot_span = (streams[0], streams[1])
    block_ranks = tract_order[0]
    positions = (
        block_ranks[:, None] * block_rows + jnp.arange(block_rows, dtype=jnp.int32)[None, :]
    ).reshape(-1)
    segments = jnp.take(segment_ids[0].reshape(-1, block_rows), block_ranks, axis=0).reshape(-1)
    allowed = (positions[None, :] <= positions[:, None]) & (segments[None, :] == segments[:, None])
    normed_span, _ = norm_parts(tokens_span.astype(jnp.float32))
    normed_in = (normed_span * gains[0] + shifts[0]).astype(jnp.bfloat16)
    projected = jnp.dot(normed_in, qkv_part, preferred_element_type=jnp.float32)
    query_shift = lax.dynamic_slice_in_dim(biases[0], here * part, part)
    value_shift = lax.dynamic_slice_in_dim(biases[1], here * part, part)
    query_heads = (
        (projected[:, :part] + query_shift).astype(jnp.bfloat16).reshape(span, heads, HEAD_DIM)
    )
    key_heads = projected[:, part : 2 * part].astype(jnp.bfloat16).reshape(span, heads, HEAD_DIM)
    value_heads = (
        (projected[:, 2 * part :] + value_shift).astype(jnp.bfloat16).reshape(span, heads, HEAD_DIM)
    )
    scores = (
        jnp.einsum("qhd,khd->hqk", query_heads, key_heads, preferred_element_type=jnp.float32)
        * attn_scale
    )
    exp_weights = jnp.where(allowed[None], jnp.exp(scores), 0.0)
    denominator = jnp.sum(exp_weights, axis=-1)
    numerator = jnp.einsum(
        "hqk,khd->qhd",
        exp_weights.astype(jnp.bfloat16),
        value_heads,
        preferred_element_type=jnp.float32,
    )
    att_heads = (numerator / denominator.T[:, :, None]).astype(jnp.bfloat16)
    log_total = jnp.log(denominator)
    att_part = att_heads.reshape(span, part)
    attended = lax.all_to_all(att_part, "ctx", 0, 1, tiled=True)
    resid_in = tokens.astype(jnp.float32)
    resid_mid = (
        resid_in + jnp.dot(attended, out_full, preferred_element_type=jnp.float32) + biases[2]
    )
    normed_two, inverse_two = norm_parts(resid_mid)
    normed_mid = lax.all_gather(
        (normed_two * gains[1] + shifts[1]).astype(jnp.bfloat16), "ctx", axis=0, tiled=True
    )
    pre_act = jnp.dot(normed_mid, up_part, preferred_element_type=jnp.float32) + up_shift
    activated, slopes = gelu_parts(pre_act)
    act_rows = activated.astype(jnp.bfloat16)
    grad_top = cotangent.astype(jnp.float32)
    grad_act = back_product(cot_span, down_part)
    grad_pre = grad_act * slopes
    grad_pre_low = grad_pre.astype(jnp.bfloat16)
    grad_norm_two = lax.psum_scatter(
        back_product(grad_pre_low, up_part).astype(jnp.bfloat16),
        "ctx",
        scatter_dimension=0,
        tiled=True,
    ).astype(jnp.float32)
    block_out = (
        resid_mid
        + lax.psum_scatter(
            jnp.dot(act_rows, down_part, preferred_element_type=jnp.float32).astype(jnp.bfloat16),
            "ctx",
            scatter_dimension=0,
            tiled=True,
        ).astype(jnp.float32)
        + biases[3]
    )
    grad_mid = grad_top + norm_back(grad_norm_two, normed_two, inverse_two, gains[1])
    mid_span = lax.all_gather(grad_mid.astype(jnp.bfloat16), "ctx", axis=0, tiled=True)
    out_rows = lax.dynamic_slice_in_dim(out_full, here * part, part)
    grad_att = back_product(mid_span, out_rows).astype(jnp.bfloat16).reshape(span, heads, HEAD_DIM)
    delta_rows = jnp.sum(grad_att.astype(jnp.float32) * att_heads.astype(jnp.float32), axis=-1).T
    soft_weights = jnp.where(allowed[None], jnp.exp(scores - log_total[:, :, None]), 0.0)
    grad_value = jnp.einsum(
        "hqk,qhd->khd",
        soft_weights.astype(jnp.bfloat16),
        grad_att,
        preferred_element_type=jnp.float32,
    ).reshape(span, part)
    grad_probs = jnp.einsum(
        "qhd,khd->hqk", grad_att, value_heads, preferred_element_type=jnp.float32
    )
    grad_scores = (soft_weights * (grad_probs - delta_rows[:, :, None])).astype(jnp.bfloat16)
    grad_query = (
        jnp.einsum(
            "hqk,khd->qhd", grad_scores, key_heads, preferred_element_type=jnp.float32
        ).reshape(span, part)
        * attn_scale
    )
    grad_key = (
        jnp.einsum(
            "hqk,qhd->khd", grad_scores, query_heads, preferred_element_type=jnp.float32
        ).reshape(span, part)
        * attn_scale
    )
    grad_proj = jnp.concatenate([grad_query, grad_key, grad_value], axis=1).astype(jnp.bfloat16)
    grad_norm_one = lax.psum_scatter(
        back_product(grad_proj, qkv_part).astype(jnp.bfloat16),
        "ctx",
        scatter_dimension=0,
        tiled=True,
    ).astype(jnp.float32)
    normed_one, inverse_one = norm_parts(resid_in)
    input_grad = grad_mid + norm_back(grad_norm_one, normed_one, inverse_one, gains[0])

    def over_dp(former, latter):
        return lax.psum_scatter(
            outer_sum(former, latter).astype(jnp.bfloat16), "dp", scatter_dimension=0, tiled=True
        )

    down_grad = over_dp(act_rows, cot_span).astype(jnp.float32)
    up_rows = over_dp(normed_mid, grad_pre_low)
    outw_rows = over_dp(att_part, mid_span)
    qkv_rows = over_dp(normed_in, grad_proj)
    outw_grad = lax.ppermute(
        outw_rows,
        both,
        [(d * ctx_count + c, c * dp_count + d) for d in range(dp_count) for c in range(ctx_count)],
    ).astype(jnp.float32)
    returned = lax.all_to_all(
        jnp.concatenate([qkv_rows, up_rows], axis=1).reshape(ctx_count, own_rows, -1),
        "ctx",
        0,
        0,
        tiled=True,
    ).astype(jnp.float32)
    qkv_grad = (
        returned[:, :, : 3 * part]
        .reshape(ctx_count, own_rows, 3, part)
        .transpose(1, 2, 0, 3)
        .reshape(own_rows, 3 * width)
    )
    up_grad = (
        returned[:, :, 3 * part :]
        .reshape(ctx_count, own_rows, dp_count, own_hidden)
        .transpose(1, 2, 0, 3)
        .reshape(own_rows, hidden * ctx_count)
    )

    def placed(sums):
        return lax.dynamic_update_slice_in_dim(
            jnp.zeros((width,), jnp.float32), sums, here * part, 0
        )

    feature_sums = jnp.stack(
        [
            jnp.sum(grad_norm_one * normed_one, axis=0),
            jnp.sum(grad_norm_two * normed_two, axis=0),
            jnp.sum(grad_norm_one, axis=0),
            jnp.sum(grad_norm_two, axis=0),
            placed(jnp.sum(grad_query, axis=0)),
            placed(jnp.sum(grad_value, axis=0)),
            jnp.sum(grad_mid, axis=0),
            jnp.sum(grad_top, axis=0),
        ]
    )
    hidden_sums = lax.dynamic_update_slice_in_dim(
        jnp.zeros((dp_count, ctx_count, own_hidden), jnp.float32),
        jnp.sum(grad_pre, axis=0).reshape(dp_count, 1, own_hidden),
        here,
        1,
    ).reshape(dp_count * ctx_count, own_hidden)
    packed = jnp.concatenate(
        [
            feature_sums.reshape(8, -1, own_feats).transpose(1, 0, 2).reshape(-1, 8 * own_feats),
            hidden_sums,
        ],
        axis=1,
    )
    owned = lax.psum_scatter(packed, both, scatter_dimension=0, tiled=True)[0]
    rows = owned[: 8 * own_feats].reshape(8, own_feats)
    return (
        block_out,
        input_grad,
        qkv_grad,
        outw_grad,
        up_grad,
        down_grad,
        rows[0:2],
        rows[2:4],
        rows[4:8],
        owned[8 * own_feats :],
    )


def solution(mesh):
    return jax.shard_map(
        shards,
        mesh=mesh,
        in_specs=(
            P(("dp", "ctx"), None),
            P(("dp", "ctx"), None),
            P("dp", None),
            P("dp", None),
            P(("dp", "ctx"), None),
            P(("dp", "ctx"), None),
            P(("dp", "ctx"), None),
            P(("dp", "ctx"), None),
            P(None, ("dp", "ctx")),
            P(None, ("dp", "ctx")),
            P(None, ("dp", "ctx")),
            P(("dp", "ctx")),
        ),
        out_specs=(
            P(("dp", "ctx"), None),
            P(("dp", "ctx"), None),
            P(("dp", "ctx"), None),
            P(("dp", "ctx"), None),
            P(("dp", "ctx"), None),
            P(("dp", "ctx"), None),
            P(None, ("dp", "ctx")),
            P(None, ("dp", "ctx")),
            P(None, ("dp", "ctx")),
            P(("dp", "ctx")),
        ),
        check_vma=False,
    )
```

profile of v0, /device:TPU:0, one launch (start us, length us, event | category | flops | bytes accessed | tf_op | source)
XLA Modules:
  0.0 666.1 jit_solution(16236123342175305526)
XLA Ops:
  11.1 13.2 %all_to_all.29 = bf16[4,32,1792]{2,1,0:T(8,128)(2,1)S(1)} all-to-all(bf16[4,32,1792]{2,1,0:T(8,128)(2,1)S(1)} %pad_maximum_fusion.2), channel_id=1, replica_groups=mesh['dp'=8,'ctx'=4] {'ctx'}, dimensions={0} | all-to-all | bytes 917504 | tf_op jit(solution)/shard_map/all_to_all | solution.py:101
  26.2 40.8 %all-gather.1 = bf16[32,1,384]{2,1,0:T(2,128)(2,1)S(1)} all-gather(bf16[1,1,384]{2,1,0:T(2,128)(2,1)S(1)} %reshape.405), channel_id=2, replica_groups=mesh['dp'=8,'ctx'=4] {'dp','ctx'}, dimensions={0}, use_global_device_ids=true | all-gather | bytes 25344 | tf_op jit(solution)/shard_map/all_gather | solution.py:79
  74.7 8.8 %all-gather.12.cloned.1.call-done = bf16[1024,768]{1,0:T(8,128)(2,1)} async-done(((bf16[128,768]{1,0:T(8,128)(2,1)}), bf16[1024,768]{1,0:T(8,128)(2,1)}) %all-gather.12.cloned.1.call-update) | async-done | bytes 1572880 | tf_op jit(solution)/shard_map/all_gather | solution.py:105
  95.3 5.7 all-to-all-done.1
  101.0 40.1 %all-gather.14.cloned.1.call-done = bf16[1024,1024]{1,0:T(8,128)(2,1)} async-done(((bf16[32,1024]{1,0:T(8,128)(2,1)}), bf16[1024,1024]{1,0:T(8,128)(2,1)}) %all-gather.14.cloned.1.call-update) | async-done | bytes 2097168 | tf_op jit(solution)/shard_map/all_gather | solution.py:106
  145.2 46.4 %all-gather.18.cloned.1.call-done = bf16[1024,1024]{1,0:T(8,128)(2,1)} async-done(((bf16[128,1024]{1,0:T(8,128)(2,1)}), bf16[1024,1024]{1,0:T(8,128)(2,1)}) %all-gather.18.cloned.1.call-update) | async-done | bytes 2097168 | tf_op jit(solution)/shard_map/all_gather | solution.py:107
  191.6 17.2 %all-gather.16.cloned.1.call-done = bf16[512,1024]{1,0:T(8,128)(2,1)} async-done(((bf16[128,1024]{1,0:T(8,128)(2,1)}), bf16[512,1024]{1,0:T(8,128)(2,1)}) %all-gather.16.cloned.1.call-update) | async-done | bytes 1048592 | tf_op jit(solution)/shard_map/all_gather | solution.py:149
  208.9 4.6 fusion.82
  213.4 46.5 %all-gather.20.cloned.1.call-done = bf16[1024,1024]{1,0:T(8,128)(2,1)} async-done(((bf16[128,1024]{1,0:T(8,128)(2,1)}), bf16[1024,1024]{1,0:T(8,128)(2,1)}) %all-gather.20.cloned.1.call-update) | async-done | bytes 2097168 | tf_op jit(solution)/shard_map/all_gather | solution.py:108
  260.0 4.8 fusion.81
  268.1 4.7 convolution_convert_fusion.5
  273.0 18.6 %reduce-scatter.10.cloned.1.call-done = bf16[128,1024]{1,0:T(8,128)(2,1)} async-done(((bf16[512,1024]{1,0:T(8,128)(2,1)}), bf16[128,1024]{1,0:T(8,128)(2,1)}) %reduce-scatter.10.cloned.1.call-update) | async-done | bytes 262160 | tf_op jit(solution)/shard_map/reduce_scatter | solution.py:159
  292.8 26.1 %reduce-scatter.8.cloned.1.call-done = bf16[128,1024]{1,0:T(8,128)(2,1)} async-done(((bf16[512,1024]{1,0:T(8,128)(2,1)}), bf16[128,1024]{1,0:T(8,128)(2,1)}) %reduce-scatter.8.cloned.1.call-update) | async-done | bytes 262160 | tf_op jit(solution)/shard_map/reduce_scatter | solution.py:167
  321.9 16.8 %all-gather.22.cloned.1.call-done = bf16[512,1024]{1,0:T(8,128)(2,1)} async-done(((bf16[128,1024]{1,0:T(8,128)(2,1)}), bf16[512,1024]{1,0:T(8,128)(2,1)}) %all-gather.22.cloned.1.call-update) | async-done | bytes 1048592 | tf_op jit(solution)/shard_map/all_gather | solution.py:176
  341.3 4.6 convolution_convert_fusion
  348.7 3.8 multiply_convert_fusion
  358.8 4.2 convolution_convert_fusion.1
  368.6 36.6 %reduce-scatter.18.cloned.1.call-done = bf16[32,1024]{1,0:T(8,128)(2,1)} async-done(((bf16[256,1024]{1,0:T(8,128)(2,1)}), bf16[32,1024]{1,0:T(8,128)(2,1)}) %reduce-scatter.18.cloned.1.call-update) | async-done | bytes 65552 | tf_op jit(solution)/shard_map/reduce_scatter | solution.py:214
  407.5 68.8 %reduce-scatter.20.cloned.1.call-done = bf16[128,1024]{1,0:T(8,128)(2,1)} async-done(((bf16[1024,1024]{1,0:T(8,128)(2,1)}), bf16[128,1024]{1,0:T(8,128)(2,1)}) %reduce-scatter.20.cloned.1.call-update) | async-done | bytes 262160 | tf_op jit(solution)/shard_map/reduce_scatter | solution.py:214
  478.7 23.7 %reduce-scatter.12.cloned.1.call-done = bf16[128,1024]{1,0:T(8,128)(2,1)} async-done(((bf16[512,1024]{1,0:T(8,128)(2,1)}), bf16[128,1024]{1,0:T(8,128)(2,1)}) %reduce-scatter.12.cloned.1.call-update) | async-done | bytes 262160 | tf_op jit(solution)/shard_map/reduce_scatter | solution.py:204
  504.3 40.7 %all-reduce = f32[32,384]{1,0:T(8,128)S(1)} all-reduce(f32[32,384]{1,0:T(8,128)S(1)} %pad_maximum_fusion.6), channel_id=10, replica_groups=mesh['dp'=8,'ctx'=4] {'dp','ctx'}, use_global_device_ids=true, to_apply=%region_28.29.clone | all-reduce | flops 12288 | bytes 98304
  545.0 30.5 %reduce-scatter.16.cloned.1.call-done = bf16[128,1024]{1,0:T(8,128)(2,1)} async-done(((bf16[1024,1024]{1,0:T(8,128)(2,1)}), bf16[128,1024]{1,0:T(8,128)(2,1)}) %reduce-scatter.16.cloned.1.call-update) | async-done | bytes 262160 | tf_op jit(solution)/shard_map/reduce_scatter | solution.py:214
  575.4 67.8 %reduce-scatter.14.cloned.1.call-done = bf16[128,768]{1,0:T(8,128)(2,1)} async-done(((bf16[1024,768]{1,0:T(8,128)(2,1)}), bf16[128,768]{1,0:T(8,128)(2,1)}) %reduce-scatter.14.cloned.1.call-update) | async-done | bytes 196624 | tf_op jit(solution)/shard_map/reduce_scatter | solution.py:214
  652.2 4.4 all-to-all-done.2
  (213 shorter events, 72.2 us)
Async XLA Ops:
  7.2 64.2 %all-gather.10.cloned.1.call-start = ((), (), s32[]{:S(2)}) async-start(), calls=%async_computation.10 | async-start | bytes 2621440 | tf_op jit(solution)/shard_map/all_gather | solution.py:104
  9.2 74.3 %all-gather.12.cloned.1.call-start = ((), (), s32[]{:S(2)}) async-start(), calls=%async_computation.11 | async-start | bytes 1769472 | tf_op jit(solution)/shard_map/all_gather | solution.py:105
  10.4 15.7 %copy-start.16 = (bf16[128]{0:T(256)(128)(2,1)S(1)}, bf16[128]{0:T(256)(128)(2,1)}, u32[]{:S(2)}) copy-start(bf16[128]{0:T(256)(128)(2,1)} %param.23) | copy-start | bytes 772
  10.7 58.0 %copy-start.15 = (s32[1,512]{1,0:T(1,128)S(1)}, s32[1,512]{1,0:T(1,128)}, u32[]{:S(2)}) copy-start(s32[1,512]{1,0:T(1,128)} %param.14) | copy-start | bytes 6148
  10.7 58.7 %copy-start.22 = (s32[1,8]{1,0:T(1,128)S(1)}, s32[1,8]{1,0:T(1,128)}, u32[]{:S(2)}) copy-start(s32[1,8]{1,0:T(1,128)} %param.15) | copy-start | bytes 100
  25.0 116.1 %all-gather.14.cloned.1.call-start = ((), (), s32[]{:S(2)}) async-start(), calls=%async_computation.12 | async-start | bytes 2162688 | tf_op jit(solution)/shard_map/all_gather | solution.py:106
  25.8 165.8 %all-gather.18.cloned.1.call-start = ((), (), s32[]{:S(2)}) async-start(), calls=%async_computation.14 | async-start | bytes 2359296 | tf_op jit(solution)/shard_map/all_gather | solution.py:107
  71.4 16.6 %copy-start.9 = (pred[512,512]{0,1:T(8,128)(4,1)}, pred[512,512]{0,1:T(8,128)(4,1)S(1)}, u32[]{:S(2)}) copy-start(pred[512,512]{0,1:T(8,128)(4,1)S(1)} %compare_and_fusion) | copy-start | bytes 786436
  89.9 51.2 %copy-start = (bf16[128,1024]{1,0:T(8,128)(2,1)S(1)}, bf16[128,1024]{1,0:T(8,128)(2,1)}, u32[]{:S(2)}) copy-start(bf16[128,1024]{1,0:T(8,128)(2,1)} %param.12) | copy-start | bytes 786436
  90.8 52.4 %copy-start.6 = (bf16[512,4,64]{0,2,1:T(8,128)(2,1)}, bf16[512,4,64]{0,2,1:T(8,128)(2,1)S(1)}, u32[]{:S(2)}) copy-start(bf16[512,4,64]{0,2,1:T(8,128)(2,1)S(1)} %fusion.37) | copy-start | bytes 786436
  91.6 9.4 %all-to-all-start.1 = ((bf16[4,128,256]{1,2,0:T(8,128)(2,1)}), bf16[4,128,256]{1,2,0:T(8,128)(2,1)S(1)}, u32[]{:S(2)}, u32[]{:S(2)}) async-start(bf16[4,128,256]{1,2,0:T(8,128)(2,1)} %copy.66), calls=%async_computation.1 | async-start | bytes 524288 | tf_op jit(solution)/shard_map/all_to_all | solution.py:143
  95.0 113.8 %all-gather.16.cloned.1.call-start = ((), (), s32[]{:S(2)}) async-start(), calls=%async_computation.13 | async-start | bytes 1310720 | tf_op jit(solution)/shard_map/all_gather | solution.py:149
  144.4 115.6 %all-gather.20.cloned.1.call-start = ((), (), s32[]{:S(2)}) async-start(), calls=%async_computation.15 | async-start | bytes 2359296 | tf_op jit(solution)/shard_map/all_gather | solution.py:108
  144.9 146.6 %reduce-scatter.10.cloned.1.call-start = ((), (), s32[]{:S(2)}) async-start(), calls=%async_computation.17 | async-start | bytes 1310720 | tf_op jit(solution)/shard_map/reduce_scatter | solution.py:159
  268.1 50.8 %reduce-scatter.8.cloned.1.call-start = ((), (), s32[]{:S(2)}) async-start(), calls=%async_computation.16 | async-start | bytes 1310720 | tf_op jit(solution)/shard_map/reduce_scatter | solution.py:167
  272.9 65.8 %all-gather.22.cloned.1.call-start = ((), (), s32[]{:S(2)}) async-start(), calls=%async_computation.18 | async-start | bytes 1310720 | tf_op jit(solution)/shard_map/all_gather | solution.py:176
  321.8 83.4 %reduce-scatter.18.cloned.1.call-start = ((), (), s32[]{:S(2)}) async-start(), calls=%async_computation.22 | async-start | bytes 589824 | tf_op jit(solution)/shard_map/reduce_scatter | solution.py:214
  341.2 135.0 %reduce-scatter.20.cloned.1.call-start = ((), (), s32[]{:S(2)}) async-start(), calls=%async_computation.23 | async-start | bytes 2359296 | tf_op jit(solution)/shard_map/reduce_scatter | solution.py:214
  345.9 156.6 %reduce-scatter.12.cloned.1.call-start = ((), (), s32[]{:S(2)}) async-start(), calls=%async_computation.19 | async-start | bytes 1310720 | tf_op jit(solution)/shard_map/reduce_scatter | solution.py:204
  358.7 216.7 %reduce-scatter.16.cloned.1.call-start = ((), (), s32[]{:S(2)}) async-start(), calls=%async_computation.21 | async-start | bytes 2359296 | tf_op jit(solution)/shard_map/reduce_scatter | solution.py:214
  363.0 280.2 %reduce-scatter.14.cloned.1.call-start = ((), (), s32[]{:S(2)}) async-start(), calls=%async_computation.20 | async-start | bytes 1769472 | tf_op jit(solution)/shard_map/reduce_scatter | solution.py:214
  405.2 72.8 %collective-permute-start = (bf16[32,1024]{1,0:T(8,128)(2,1)}, bf16[32,1024]{1,0:T(8,128)(2,1)S(1)}, u32[]{:S(2)}, u32[]{:S(2)}) collective-permute-start(bf16[32,1024]{1,0:T(8,128)(2,1)} %reduce-scatter.18.cloned.1.call-done), channel_id=1, source_target_pairs={{0,0},{1,8},{2,16},{3,24},{4,1},{5,9},{6,17},{7,25},{8,2},{9,10},{... | collective-permute-start | bytes 196616 | tf_op jit(solution)/shard_map/ppermute | solution.py:222
  502.5 148.7 %copy-start.8 = (bf16[128,1024]{1,0:T(8,128)(2,1)S(1)}, bf16[128,1024]{1,0:T(8,128)(2,1)}, u32[]{:S(2)}) copy-start(bf16[128,1024]{1,0:T(8,128)(2,1)} %reduce-scatter.12.cloned.1.call-done) | copy-start | bytes 786436
  645.0 11.6 %all-to-all-start.2 = ((bf16[4,32,1792]{2,1,0:T(8,128)(2,1)}), bf16[4,32,1792]{2,1,0:T(8,128)(2,1)S(1)}, u32[]{:S(2)}, u32[]{:S(2)}) async-start(bf16[4,32,1792]{2,1,0:T(8,128)(2,1)} %bitcast.30), calls=%async_computation.7 | async-start | bytes 917504 | tf_op jit(solution)/shard_map/all_to_all | solution.py:227
  (20 other events, 92.8 us)
Sparse Core Ops, SparseCore 0:
  10.1 25.9 all-gather.9
  38.8 44.5 all-gather.11
  86.3 54.7 all-gather.13
  143.6 47.9 all-gather.17
  193.6 15.2 all-gather.15
  210.8 49.0 all-gather.19
  268.2 23.2 reduce-scatter.9
  294.1 24.7 reduce-scatter.7
  321.9 16.6 all-gather.21
  342.4 62.7 reduce-scatter.17
  408.8 67.4 reduce-scatter.19
  478.6 23.7 reduce-scatter.11
  506.0 69.3 reduce-scatter.15
  578.7 64.4 reduce-scatter.13
where the time goes:
time: 667 us; the launch traced here: 666 us
  waiting for transfers between devices  459 us (69%)
  blocking collectives  94.7 us (14%)
  matrix products  47.9 us (7%)
  local copies, waits for them, and re-layouts  20.1 us (3%)
  other arithmetic  20 us (3%)
  between operations  14.6 us (2%)
  starting transfers between devices  9.33 us (1%)
    reduce_scatter x4, waiting for transfers between devices, over_dp(): lax.psum_scatter(outer_sum(former, latter).astype(jnp.bfloat16), 'dp', sc...  204 us
    all_gather x1, waiting for transfers between devices, shards(): down_part = lax.all_gather(down_weight, 'dp', axis=0, tiled=True)  46.5 us
    all_gather x1, waiting for transfers between devices, shards(): up_part = lax.all_gather(swapped[:, 3 * part:], 'dp', axis=0, tiled=True)  46.4 us
    all_gather x1, blocking collectives, shards(): lax.all_gather(smalls, both, axis=0, tiled=True).astype(jnp.float32)  40.8 us
    unnamed x1, blocking collectives  40.7 us
    all_gather x1, waiting for transfers between devices, shards(): out_full = lax.all_gather(out_weight, both, axis=0, tiled=True)  40.1 us
    reduce_scatter x1, waiting for transfers between devices, shards(): lax.psum_scatter(jnp.dot(act_rows, down_part, preferred_element_type=jnp....  26.1 us
    reduce_scatter x1, waiting for transfers between devices, shards(): lax.psum_scatter(back_product(grad_proj, qkv_part).astype(jnp.bfloat16),...  23.7 us
  transfers between devices with their start and end apart: 17, of which 15 were waited for; matrix products, arithmetic and copies ran while one was open for 10% of the time, Pallas kernels for 0%

commit v1 on v0

--- a/solution.py
+++ b/solution.py
@@ -6,6 +6,28 @@
 HEAD_DIM = 64
 EPSILON = 1e-05
 GELU_COEF = 0.7978845608028654
+
+
+def joined_along(parts, dim):
+    parts = jnp.moveaxis(parts, 0, dim)
+    lengths = parts.shape
+    return parts.reshape(*lengths[:dim], lengths[dim] * lengths[dim + 1], *lengths[dim + 2 :])
+
+
+def gather_around(x, axis, dim):
+    peers = lax.axis_size(axis)
+    pairs = [(i, (i + 1) % peers) for i in range(peers)]
+    back = [(b, a) for a, b in pairs]
+    lower, upper = ([], [])
+    for step in range(peers - 1):
+        if step % 2 == 0:
+            lower.append(lax.ppermute(lower[-1] if lower else x, axis, pairs))
+        else:
+            upper.append(lax.ppermute(upper[-1] if upper else x, axis, back))
+    tiles = jnp.stack([*lower[::-1], x, *upper])
+    shift = lax.axis_index(axis) - len(lower)
+    tiles = tiles[(jnp.arange(peers) - shift) % peers]
+    return joined_along(tiles, dim)
 
 
 def gelu_parts(inputs):
@@ -104,7 +126,7 @@
     streams = lax.all_gather(jnp.stack([tokens, cotangent]), "ctx", axis=1, tiled=True)
     qkv_part = lax.all_gather(swapped[:, : 3 * part], "dp", axis=0, tiled=True)
     out_full = lax.all_gather(out_weight, both, axis=0, tiled=True)
-    up_part = lax.all_gather(swapped[:, 3 * part :], "dp", axis=0, tiled=True)
+    up_part = gather_around(swapped[:, 3 * part :], "dp", 0)
     down_part = lax.all_gather(down_weight, "dp", axis=0, tiled=True)
     tokens_span, cot_span = (streams[0], streams[1])
     block_ranks = tract_order[0]

time: 667 us -> 629 us (0.943)
  waiting for transfers between devices: 459 us -> 395 us
  starting transfers between devices: 9.33 us -> 29.1 us
    all_gather x1 -> x0, waiting for transfers between devices: 46.4 us -> none  [shards(): up_part = lax.all_gather(swapped[:, 3 * part:], 'dp', axis=0, tiled=True)]
    all_gather x1, waiting for transfers between devices: 46.5 us -> 14.3 us  [shards(): down_part = lax.all_gather(down_weight, 'dp', axis=0, tiled=True)]
    ppermute x0 -> x7, waiting for transfers between devices: none -> 31.2 us  [the longest x4 31.2 us: gather_around(): lower.append(lax.ppermute(lower[-1] if lower else x, axis, pairs))]
    ppermute x0 -> x7, starting transfers between devices: none -> 20 us  [the longest x3 13.5 us: gather_around(): upper.append(lax.ppermute(upper[-1] if upper else x, axis, back))]
    all_gather x1, waiting for transfers between devices: 17.2 us -> 0.01 us  [shards(): lax.all_gather((normed_two * gains[1] + shifts[1]).astype(jnp.bfloat16),...]
  transfers between devices with their start and end apart: 17 -> 23, of which waited for: 15 -> 17; matrix products, arithmetic and copies ran while one was open for 10% -> 11% of each run, Pallas kernels for 0% -> 0%
where the time goes in v1:
time: 629 us; the launch traced here: 628 us
  waiting for transfers between devices  395 us (63%)
  blocking collectives  94.8 us (15%)
  matrix products  48.1 us (8%)
  starting transfers between devices  29.1 us (5%)
  local copies, waits for them, and re-layouts  26.4 us (4%)
  other arithmetic  20 us (3%)
  between operations  14.7 us (2%)
    reduce_scatter x4, waiting for transfers between devices, over_dp(): lax.psum_scatter(outer_sum(former, latter).astype(jnp.bfloat16), 'dp', sc...  203 us
    all_gather x1, blocking collectives, shards(): lax.all_gather(smalls, both, axis=0, tiled=True).astype(jnp.float32)  40.8 us
    unnamed x1, blocking collectives  40.7 us
    all_gather x1, waiting for transfers between devices, shards(): out_full = lax.all_gather(out_weight, both, axis=0, tiled=True)  40.1 us
    ppermute x4, waiting for transfers between devices, gather_around(): lower.append(lax.ppermute(lower[-1] if lower else x, axis, pairs))  31.2 us
    reduce_scatter x1, waiting for transfers between devices, shards(): lax.psum_scatter(jnp.dot(act_rows, down_part, preferred_element_type=jnp....  26.1 us
    reduce_scatter x1, waiting for transfers between devices, shards(): lax.psum_scatter(back_product(grad_proj, qkv_part).astype(jnp.bfloat16),...  24 us
    reduce_scatter x1, waiting for transfers between devices, shards(): lax.psum_scatter(back_product(grad_pre_low, up_part).astype(jnp.bfloat16)...  18.6 us
  transfers between devices with their start and end apart: 23, of which 17 were waited for; matrix products, arithmetic and copies ran while one was open for 11% of the time, Pallas kernels for 0%

profile of v1, /device:TPU:0, one launch (start us, length us, event | category | flops | bytes accessed | tf_op | source)
XLA Modules:
  0.0 628.2 jit_solution(12731028794834879494)
XLA Ops:
  11.1 13.2 %all_to_all.29 = bf16[4,32,1792]{2,1,0:T(8,128)(2,1)S(1)} all-to-all(bf16[4,32,1792]{2,1,0:T(8,128)(2,1)S(1)} %pad_maximum_fusion.2), channel_id=1, replica_groups=mesh['dp'=8,'ctx'=4] {'ctx'}, dimensions={0} | all-to-all | bytes 917504 | tf_op jit(solution)/shard_map/all_to_all | solution.py:123
  26.1 40.8 %all-gather.1 = bf16[32,1,384]{2,1,0:T(2,128)(2,1)S(1)} all-gather(bf16[1,1,384]{2,1,0:T(2,128)(2,1)S(1)} %reshape.466), channel_id=2, replica_groups=mesh['dp'=8,'ctx'=4] {'dp','ctx'}, dimensions={0}, use_global_device_ids=true | all-gather | bytes 25344 | tf_op jit(solution)/shard_map/all_gather | solution.py:101
  73.9 9.6 %all-gather.11.cloned.1.call-done = bf16[1024,768]{1,0:T(8,128)(2,1)} async-done(((bf16[128,768]{1,0:T(8,128)(2,1)}), bf16[1024,768]{1,0:T(8,128)(2,1)}) %all-gather.11.cloned.1.call-update) | async-done | bytes 1572880 | tf_op jit(solution)/shard_map/all_gather | solution.py:127
  95.3 5.7 all-to-all-done.1
  101.0 40.1 %all-gather.13.cloned.1.call-done = bf16[1024,1024]{1,0:T(8,128)(2,1)} async-done(((bf16[32,1024]{1,0:T(8,128)(2,1)}), bf16[1024,1024]{1,0:T(8,128)(2,1)}) %all-gather.13.cloned.1.call-update) | async-done | bytes 2097168 | tf_op jit(solution)/shard_map/all_gather | solution.py:128
  146.5 9.7 %collective-permute-done = bf16[128,1024]{1,0:T(8,128)(2,1)S(1)} collective-permute-done((bf16[128,1024]{1,0:T(8,128)(2,1)S(1)}, bf16[128,1024]{1,0:T(8,128)(2,1)S(1)}, u32[]{:S(2)}, u32[]{:S(2)}) %collective-permute-start) | collective-permute-done | bytes 262176 | tf_op jit(solution)/shard_map/ppermute | solution.py:24
  156.2 4.7 collective-permute-start.4
  160.9 6.3 collective-permute-done.1
  169.7 5.8 collective-permute-start.5
  175.4 7.9 %collective-permute-done.2 = bf16[128,1024]{1,0:T(8,128)(2,1)S(1)} collective-permute-done((bf16[128,1024]{1,0:T(8,128)(2,1)S(1)}, bf16[128,1024]{1,0:T(8,128)(2,1)S(1)}, u32[]{:S(2)}, u32[]{:S(2)}) %collective-permute-start.2) | collective-permute-done | bytes 262176 | tf_op jit(solution)/shard_map/ppermute | solution.py:24
  188.9 7.4 %collective-permute-done.3 = bf16[128,1024]{1,0:T(8,128)(2,1)} collective-permute-done((bf16[128,1024]{1,0:T(8,128)(2,1)S(1)}, bf16[128,1024]{1,0:T(8,128)(2,1)}, u32[]{:S(2)}, u32[]{:S(2)}) %collective-permute-start.3) | collective-permute-done | bytes 262176 | tf_op jit(solution)/shard_map/ppermute | solution.py:24
  203.4 4.7 fusion.84
  208.1 14.3 %all-gather.17.cloned.1.call-done = bf16[1024,1024]{1,0:T(8,128)(2,1)} async-done(((bf16[128,1024]{1,0:T(8,128)(2,1)}), bf16[1024,1024]{1,0:T(8,128)(2,1)}) %all-gather.17.cloned.1.call-update) | async-done | bytes 2097168 | tf_op jit(solution)/shard_map/all_gather | solution.py:130
  222.4 4.7 fusion.83
  230.5 4.7 convolution_convert_fusion.5
  235.4 18.6 %reduce-scatter.10.cloned.1.call-done = bf16[128,1024]{1,0:T(8,128)(2,1)} async-done(((bf16[512,1024]{1,0:T(8,128)(2,1)}), bf16[128,1024]{1,0:T(8,128)(2,1)}) %reduce-scatter.10.cloned.1.call-update) | async-done | bytes 262160 | tf_op jit(solution)/shard_map/reduce_scatter | solution.py:181
  255.2 26.1 %reduce-scatter.8.cloned.1.call-done = bf16[128,1024]{1,0:T(8,128)(2,1)} async-done(((bf16[512,1024]{1,0:T(8,128)(2,1)}), bf16[128,1024]{1,0:T(8,128)(2,1)}) %reduce-scatter.8.cloned.1.call-update) | async-done | bytes 262160 | tf_op jit(solution)/shard_map/reduce_scatter | solution.py:189
  284.3 16.8 %all-gather.19.cloned.1.call-done = bf16[512,1024]{1,0:T(8,128)(2,1)} async-done(((bf16[128,1024]{1,0:T(8,128)(2,1)}), bf16[512,1024]{1,0:T(8,128)(2,1)}) %all-gather.19.cloned.1.call-update) | async-done | bytes 1048592 | tf_op jit(solution)/shard_map/all_gather | solution.py:198
  331.1 36.6 %reduce-scatter.18.cloned.1.call-done = bf16[32,1024]{1,0:T(8,128)(2,1)} async-done(((bf16[256,1024]{1,0:T(8,128)(2,1)}), bf16[32,1024]{1,0:T(8,128)(2,1)}) %reduce-scatter.18.cloned.1.call-update) | async-done | bytes 65552 | tf_op jit(solution)/shard_map/reduce_scatter | solution.py:236
  369.9 68.5 %reduce-scatter.20.cloned.1.call-done = bf16[128,1024]{1,0:T(8,128)(2,1)} async-done(((bf16[1024,1024]{1,0:T(8,128)(2,1)}), bf16[128,1024]{1,0:T(8,128)(2,1)}) %reduce-scatter.20.cloned.1.call-update) | async-done | bytes 262160 | tf_op jit(solution)/shard_map/reduce_scatter | solution.py:236
  440.9 24.0 %reduce-scatter.12.cloned.1.call-done = bf16[128,1024]{1,0:T(8,128)(2,1)} async-done(((bf16[512,1024]{1,0:T(8,128)(2,1)}), bf16[128,1024]{1,0:T(8,128)(2,1)}) %reduce-scatter.12.cloned.1.call-update) | async-done | bytes 262160 | tf_op jit(solution)/shard_map/reduce_scatter | solution.py:226
  466.7 40.7 %all-reduce = f32[32,384]{1,0:T(8,128)S(1)} all-reduce(f32[32,384]{1,0:T(8,128)S(1)} %pad_maximum_fusion.6), channel_id=10, replica_groups=mesh['dp'=8,'ctx'=4] {'dp','ctx'}, use_global_device_ids=true, to_apply=%region_28.29.clone | all-reduce | flops 12288 | bytes 98304
  507.4 29.9 %reduce-scatter.16.cloned.1.call-done = bf16[128,1024]{1,0:T(8,128)(2,1)} async-done(((bf16[1024,1024]{1,0:T(8,128)(2,1)}), bf16[128,1024]{1,0:T(8,128)(2,1)}) %reduce-scatter.16.cloned.1.call-update) | async-done | bytes 262160 | tf_op jit(solution)/shard_map/reduce_scatter | solution.py:236
  537.3 68.0 %reduce-scatter.14.cloned.1.call-done = bf16[128,768]{1,0:T(8,128)(2,1)} async-done(((bf16[1024,768]{1,0:T(8,128)(2,1)}), bf16[128,768]{1,0:T(8,128)(2,1)}) %reduce-scatter.14.cloned.1.call-update) | async-done | bytes 196624 | tf_op jit(solution)/shard_map/reduce_scatter | solution.py:236
  (247 shorter events, 104.8 us)
Async XLA Ops:
  7.2 63.4 %all-gather.9.cloned.1.call-start = ((), (), s32[]{:S(2)}) async-start(), calls=%async_computation.10 | async-start | bytes 2621440 | tf_op jit(solution)/shard_map/all_gather | solution.py:126
  9.2 74.3 %all-gather.11.cloned.1.call-start = ((), (), s32[]{:S(2)}) async-start(), calls=%async_computation.11 | async-start | bytes 1769472 | tf_op jit(solution)/shard_map/all_gather | solution.py:127
  25.0 116.1 %all-gather.13.cloned.1.call-start = ((), (), s32[]{:S(2)}) async-start(), calls=%async_computation.12 | async-start | bytes 2162688 | tf_op jit(solution)/shard_map/all_gather | solution.py:128
  91.6 9.4 %all-to-all-start.1 = ((bf16[4,128,256]{1,2,0:T(8,128)(2,1)}), bf16[4,128,256]{1,2,0:T(8,128)(2,1)S(1)}, u32[]{:S(2)}, u32[]{:S(2)}) async-start(bf16[4,128,256]{1,2,0:T(8,128)(2,1)} %copy.66), calls=%async_computation.1 | async-start | bytes 524288 | tf_op jit(solution)/shard_map/all_to_all | solution.py:165
  95.0 108.4 %all-gather.15.cloned.1.call-start = ((), (), s32[]{:S(2)}) async-start(), calls=%async_computation.13 | async-start | bytes 1310720 | tf_op jit(solution)/shard_map/all_gather | solution.py:171
  144.3 78.0 %all-gather.17.cloned.1.call-start = ((), (), s32[]{:S(2)}) async-start(), calls=%async_computation.14 | async-start | bytes 2359296 | tf_op jit(solution)/shard_map/all_gather | solution.py:130
  144.9 109.0 %reduce-scatter.10.cloned.1.call-start = ((), (), s32[]{:S(2)}) async-start(), calls=%async_computation.16 | async-start | bytes 1310720 | tf_op jit(solution)/shard_map/reduce_scatter | solution.py:181
  145.0 11.2 %collective-permute-start = (bf16[128,1024]{1,0:T(8,128)(2,1)S(1)}, bf16[128,1024]{1,0:T(8,128)(2,1)S(1)}, u32[]{:S(2)}, u32[]{:S(2)}) collective-permute-start(bf16[128,1024]{1,0:T(8,128)(2,1)S(1)} %slice.151), channel_id=1, source_target_pairs={{0,4},{4,8},{8,12},{12,16},{16,20},{20,24},{24,28},{28,0},{1,5},{5... | collective-permute-start | bytes 786440 | tf_op jit(solution)/shard_map/ppermute | solution.py:24
  156.2 11.0 %collective-permute-start.1 = (bf16[128,1024]{1,0:T(8,128)(2,1)S(1)}, bf16[128,1024]{1,0:T(8,128)(2,1)S(1)}, u32[]{:S(2)}, u32[]{:S(2)}) collective-permute-start(bf16[128,1024]{1,0:T(8,128)(2,1)S(1)} %collective-permute-done), channel_id=1, source_target_pairs={{0,4},{4,8},{8,12},{12,16},{16,20},{20,24},{24,28},{28,0},{1,5},{5... | collective-permute-start | bytes 786440 | tf_op jit(solution)/shard_map/ppermute | solution.py:24
  156.2 13.5 %collective-permute-start.4 = (bf16[128,1024]{1,0:T(8,128)(2,1)S(1)}, bf16[128,1024]{1,0:T(8,128)(2,1)S(1)}, u32[]{:S(2)}, u32[]{:S(2)}) collective-permute-start(bf16[128,1024]{1,0:T(8,128)(2,1)S(1)} %slice.151), channel_id=1, source_target_pairs={{4,0},{8,4},{12,8},{16,12},{20,16},{24,20},{28,24},{0,28},{5,1},{9... | collective-permute-start | bytes 786440 | tf_op jit(solution)/shard_map/ppermute | solution.py:26
  167.2 16.1 %collective-permute-start.2 = (bf16[128,1024]{1,0:T(8,128)(2,1)S(1)}, bf16[128,1024]{1,0:T(8,128)(2,1)S(1)}, u32[]{:S(2)}, u32[]{:S(2)}) collective-permute-start(bf16[128,1024]{1,0:T(8,128)(2,1)S(1)} %collective-permute-done.1), channel_id=1, source_target_pairs={{0,4},{4,8},{8,12},{12,16},{16,20},{20,24},{24,28},{28,0},{1,5},{5... | collective-permute-start | bytes 786440 | tf_op jit(solution)/shard_map/ppermute | solution.py:24
  169.7 16.2 %collective-permute-start.5 = (bf16[128,1024]{1,0:T(8,128)(2,1)S(1)}, bf16[128,1024]{1,0:T(8,128)(2,1)}, u32[]{:S(2)}, u32[]{:S(2)}) collective-permute-start(bf16[128,1024]{1,0:T(8,128)(2,1)S(1)} %collective-permute-done.4), channel_id=1, source_target_pairs={{4,0},{8,4},{12,8},{16,12},{20,16},{24,20},{28,24},{0,28},{5,1},{9... | collective-permute-start | bytes 786440 | tf_op jit(solution)/shard_map/ppermute | solution.py:26
  183.3 13.0 %collective-permute-start.3 = (bf16[128,1024]{1,0:T(8,128)(2,1)S(1)}, bf16[128,1024]{1,0:T(8,128)(2,1)}, u32[]{:S(2)}, u32[]{:S(2)}) collective-permute-start(bf16[128,1024]{1,0:T(8,128)(2,1)S(1)} %collective-permute-done.2), channel_id=1, source_target_pairs={{0,4},{4,8},{8,12},{12,16},{16,20},{20,24},{24,28},{28,0},{1,5},{5... | collective-permute-start | bytes 786440 | tf_op jit(solution)/shard_map/ppermute | solution.py:24
  185.9 15.5 %collective-permute-start.6 = (bf16[128,1024]{1,0:T(8,128)(2,1)}, bf16[128,1024]{1,0:T(8,128)(2,1)S(1)}, u32[]{:S(2)}, u32[]{:S(2)}) collective-permute-start(bf16[128,1024]{1,0:T(8,128)(2,1)} %collective-permute-done.5), channel_id=1, source_target_pairs={{4,0},{8,4},{12,8},{16,12},{20,16},{24,20},{28,24},{0,28},{5,1},{9... | collective-permute-start | bytes 786440 | tf_op jit(solution)/shard_map/ppermute | solution.py:26
  230.5 50.8 %reduce-scatter.8.cloned.1.call-start = ((), (), s32[]{:S(2)}) async-start(), calls=%async_computation.15 | async-start | bytes 1310720 | tf_op jit(solution)/shard_map/reduce_scatter | solution.py:189
  235.2 65.8 %all-gather.19.cloned.1.call-start = ((), (), s32[]{:S(2)}) async-start(), calls=%async_computation.17 | async-start | bytes 1310720 | tf_op jit(solution)/shard_map/all_gather | solution.py:198
  284.2 83.5 %reduce-scatter.18.cloned.1.call-start = ((), (), s32[]{:S(2)}) async-start(), calls=%async_computation.21 | async-start | bytes 589824 | tf_op jit(solution)/shard_map/reduce_scatter | solution.py:236
  303.7 134.8 %reduce-scatter.20.cloned.1.call-start = ((), (), s32[]{:S(2)}) async-start(), calls=%async_computation.22 | async-start | bytes 2359296 | tf_op jit(solution)/shard_map/reduce_scatter | solution.py:236
  308.3 156.6 %reduce-scatter.12.cloned.1.call-start = ((), (), s32[]{:S(2)}) async-start(), calls=%async_computation.18 | async-start | bytes 1310720 | tf_op jit(solution)/shard_map/reduce_scatter | solution.py:226
  321.1 216.2 %reduce-scatter.16.cloned.1.call-start = ((), (), s32[]{:S(2)}) async-start(), calls=%async_computation.20 | async-start | bytes 2359296 | tf_op jit(solution)/shard_map/reduce_scatter | solution.py:236
  325.4 279.9 %reduce-scatter.14.cloned.1.call-start = ((), (), s32[]{:S(2)}) async-start(), calls=%async_computation.19 | async-start | bytes 1769472 | tf_op jit(solution)/shard_map/reduce_scatter | solution.py:236
  367.7 72.5 %collective-permute-start.7 = (bf16[32,1024]{1,0:T(8,128)(2,1)}, bf16[32,1024]{1,0:T(8,128)(2,1)S(1)}, u32[]{:S(2)}, u32[]{:S(2)}) collective-permute-start(bf16[32,1024]{1,0:T(8,128)(2,1)} %reduce-scatter.18.cloned.1.call-done), channel_id=1, source_target_pairs={{0,0},{1,8},{2,16},{3,24},{4,1},{5,9},{6,17},{7,25},{8,2},{9,10},{... | collective-permute-start | bytes 196616 | tf_op jit(solution)/shard_map/ppermute | solution.py:244
  464.9 148.3 %copy-start.10 = (bf16[128,1024]{1,0:T(8,128)(2,1)S(1)}, bf16[128,1024]{1,0:T(8,128)(2,1)}, u32[]{:S(2)}) copy-start(bf16[128,1024]{1,0:T(8,128)(2,1)} %reduce-scatter.12.cloned.1.call-done) | copy-start | bytes 786436
  607.1 11.6 %all-to-all-start.2 = ((bf16[4,32,1792]{2,1,0:T(8,128)(2,1)}), bf16[4,32,1792]{2,1,0:T(8,128)(2,1)S(1)}, u32[]{:S(2)}, u32[]{:S(2)}) async-start(bf16[4,32,1792]{2,1,0:T(8,128)(2,1)} %bitcast.40), calls=%async_computation.7 | async-start | bytes 917504 | tf_op jit(solution)/shard_map/all_to_all | solution.py:249
  (32 other events, 448.9 us)
Sparse Core Ops, SparseCore 0:
  10.1 25.9 all-gather.8
  38.9 44.5 all-gather.10
  86.3 54.7 all-gather.12
  144.5 15.5 all-gather.14
  162.0 60.3 all-gather.16
  230.6 23.3 reduce-scatter.9
  256.5 24.7 reduce-scatter.7
  284.3 16.6 all-gather.18
  305.0 62.6 reduce-scatter.17
  371.1 67.3 reduce-scatter.19
  441.0 23.8 reduce-scatter.11
  468.3 68.9 reduce-scatter.15
  540.7 64.5 reduce-scatter.13
